TPU v7x, 256 devices: a whole 4x4x8 slice. The times are simulated.
256 devices in a mesh: row: 32 (over y, z), col: 8 (over x, core).
Axes of the slice: x: 4, y: 4, z: 8, core: 2. Of those that a mesh axis runs over, the one named last changes fastest.
Arguments:
- acts: bfloat16 [6144, 28672], P('col', 'row'), may hold values from -12 to 12
- out_grad: bfloat16 [6144, 8192], P('row', 'col'), may hold values from -12 to 12
- lengths: int32 [8], replicated, may hold values from 1 to 768, 4800 in all
Outputs:
- weight_grad: bfloat16 [28672, 8192], P('row', 'col')
- norms: float32 [8], replicated
All inputs are finite; a program needn't handle non-finite values.
Results may differ from a plain program's by a relative error of at most 0.0013.
Values may be sent and summed in bfloat16 or wider, within the bound.
No kernel may reach another device: no remote copies, remote signals or barrier semaphores. Data moves between devices by JAX's collectives and lax.ppermute only.
A program may use at most 128 MiB of HBM per device.

v0:
```python
import jax
import jax.numpy as jnp
from jax import lax
from jax.sharding import PartitionSpec as P

FF = 28672
D = 8192


def body(acts, out_grad, lengths):
    n_row = lax.axis_size("row")
    own_rows = out_grad.shape[0]
    tokens = own_rows * n_row
    seqs = lengths.shape[0]
    seq_len = tokens // seqs
    slot = lax.broadcasted_iota(jnp.int32, (seq_len, 1), 0)
    act_full = lax.all_gather(acts, "col", axis=0, tiled=True)
    grad_full = lax.all_gather(out_grad, "row", axis=0, tiled=True)
    products = []
    locals_ = []
    for seq in range(seqs):
        act_rows = act_full[seq * seq_len : (seq + 1) * seq_len]
        grad_rows = grad_full[seq * seq_len : (seq + 1) * seq_len]
        grad_rows = jnp.where(slot < lengths[seq], grad_rows, jnp.zeros_like(grad_rows))
        product = lax.dot_general(
            act_rows, grad_rows, (((0,), (0,)), ((), ())), preferred_element_type=jnp.float32
        )
        products.append(product)
        locals_.append(jnp.sum(product * product))
    squares = lax.psum(jnp.stack(locals_), ("row", "col"))
    divisor = float(FF) * float(D) * float(seq_len)
    norms = jnp.sqrt(squares / divisor)
    scale = 1.0 / (norms + 0.1)
    total = scale[0] * products[0]
    for seq in range(1, seqs):
        total = total + scale[seq] * products[seq]
    weight_grad = (total / jnp.sqrt(jnp.float32(tokens))).astype(jnp.bfloat16)
    return (weight_grad, norms)


def solution(mesh):
    placed = (P("col", "row"), P("row", "col"), P())
    return jax.shard_map(
        body, mesh=mesh, in_specs=placed, out_specs=(P("row", "col"), P()), check_vma=False
    )
```

profile of v0, /device:TPU:1, one launch (start us, length us, event | category | flops | bytes accessed | tf_op | source)
XLA Modules:
  0.0 344.8 jit_solution(8986895510977710011)
XLA Ops:
  7.2 0.0 all-gather.5.cloned.1.call-start
  7.2 0.7 all-gather.5.cloned.1.call-update
  7.9 0.0 all-gather.3.cloned.1.call-start
  7.9 0.7 all-gather.3.cloned.1.call-update
  8.6 1.6 fusion.42
  10.3 0.7 iota_compare_fusion.1
  10.9 0.7 iota_compare_fusion.2
  11.6 0.6 iota_compare_fusion.3
  12.2 0.7 iota_compare_fusion.4
  12.9 0.6 iota_compare_fusion.5
  13.5 0.6 iota_compare_fusion.6
  14.1 0.6 iota_compare_fusion.7
  14.8 0.6 iota_compare_fusion
  15.3 62.0 %all-gather.5.cloned.1.call-done = bf16[6144,896]{1,0:T(8,128)(2,1)} async-done(((bf16[768,896]{1,0:T(8,128)(2,1)}), bf16[6144,896]{1,0:T(8,128)(2,1)}) %all-gather.5.cloned.1.call-update) | async-done | bytes 11010064 | tf_op jit(solution)/shard_map/all_gather | solution.py:17
  77.3 121.9 %all-gather.3.cloned.1.call-done = bf16[6144,1024]{1,0:T(8,128)(2,1)} async-done(((bf16[192,1024]{1,0:T(8,128)(2,1)}), bf16[6144,1024]{1,0:T(8,128)(2,1)}) %all-gather.3.cloned.1.call-update) | async-done | bytes 12582928 | tf_op jit(solution)/shard_map/all_gather | solution.py:18
  199.2 0.0 copy-start
  199.2 6.4 %multiply_reduce_fusion = (f32[]{:T(128)}, f32[1024,896]{1,0:T(8,128)}) fusion(bf16[6144,896]{1,0:T(8,128)(2,1)} %all-gather.5.cloned.1.call-done, bf16[6144,1024]{1,0:T(8,128)(2,1)} %all-gather.3.cloned.1.call-done, pred[768]{0:T(1024)(128)(4,1)S(1)} %iota_compare_fusion), kind=kOutput, calls=%fused_computation.1 | convolution fusion | flops 1411907584 | bytes 6619908 | tf_op jit(solution)/shard_map/dot_general | solution.py:25
  205.6 0.4 copy-done
  206.0 0.0 copy-start.1
  206.0 5.9 %multiply_reduce_fusion.7 = (f32[]{:T(128)}, f32[1024,896]{1,0:T(8,128)}) fusion(bf16[6144,896]{1,0:T(8,128)(2,1)} %all-gather.5.cloned.1.call-done, bf16[6144,1024]{1,0:T(8,128)(2,1)S(1)} %copy-done, pred[768]{0:T(1024)(128)(4,1)S(1)} %iota_compare_fusion.7), kind=kOutput, calls=%fused_computation.8 | convolution fusion | flops 1411907584 | bytes 6620164 | tf_op jit(solution)/shard_map/dot_general | solution.py:25
  211.8 0.0 copy-done.1
  211.8 4.5 %multiply_reduce_fusion.6 = (f32[]{:T(128)}, f32[1024,896]{1,0:T(8,128)}) fusion(bf16[6144,896]{1,0:T(8,128)(2,1)S(1)} %copy-done.1, bf16[6144,1024]{1,0:T(8,128)(2,1)S(1)} %copy-done, pred[768]{0:T(1024)(128)(4,1)S(1)} %iota_compare_fusion.6), kind=kOutput, calls=%fused_computation.7 | convolution fusion | flops 1411907584 | bytes 6620164 | tf_op jit(solution)/shard_map/dot_general | solution.py:25
  216.3 4.5 %multiply_reduce_fusion.5 = (f32[]{:T(128)}, f32[1024,896]{1,0:T(8,128)}) fusion(bf16[6144,896]{1,0:T(8,128)(2,1)S(1)} %copy-done.1, bf16[6144,1024]{1,0:T(8,128)(2,1)S(1)} %copy-done, pred[768]{0:T(1024)(128)(4,1)S(1)} %iota_compare_fusion.5), kind=kOutput, calls=%fused_computation.6 | convolution fusion | flops 1411907584 | bytes 6620164 | tf_op jit(solution)/shard_map/dot_general | solution.py:25
  220.8 4.5 %multiply_reduce_fusion.4 = (f32[]{:T(128)}, f32[1024,896]{1,0:T(8,128)}) fusion(bf16[6144,896]{1,0:T(8,128)(2,1)S(1)} %copy-done.1, bf16[6144,1024]{1,0:T(8,128)(2,1)S(1)} %copy-done, pred[768]{0:T(1024)(128)(4,1)S(1)} %iota_compare_fusion.4), kind=kOutput, calls=%fused_computation.5 | convolution fusion | flops 1411907584 | bytes 6620164 | tf_op jit(solution)/shard_map/dot_general | solution.py:25
  225.3 4.4 %multiply_reduce_fusion.3 = (f32[]{:T(128)}, f32[1024,896]{1,0:T(8,128)}) fusion(bf16[6144,896]{1,0:T(8,128)(2,1)S(1)} %copy-done.1, bf16[6144,1024]{1,0:T(8,128)(2,1)S(1)} %copy-done, pred[768]{0:T(1024)(128)(4,1)S(1)} %iota_compare_fusion.3), kind=kOutput, calls=%fused_computation.4 | convolution fusion | flops 1411907584 | bytes 6620164 | tf_op jit(solution)/shard_map/dot_general | solution.py:25
  229.8 4.6 %multiply_reduce_fusion.2 = (f32[]{:T(128)}, f32[1024,896]{1,0:T(8,128)}) fusion(bf16[6144,896]{1,0:T(8,128)(2,1)S(1)} %copy-done.1, bf16[6144,1024]{1,0:T(8,128)(2,1)S(1)} %copy-done, pred[768]{0:T(1024)(128)(4,1)S(1)} %iota_compare_fusion.2), kind=kOutput, calls=%fused_computation.3 | convolution fusion | flops 1411907584 | bytes 6620164 | tf_op jit(solution)/shard_map/dot_general | solution.py:25
  234.4 4.5 %multiply_reduce_fusion.1 = (f32[]{:T(128)}, f32[1024,896]{1,0:T(8,128)}) fusion(bf16[6144,896]{1,0:T(8,128)(2,1)S(1)} %copy-done.1, bf16[6144,1024]{1,0:T(8,128)(2,1)S(1)} %copy-done, pred[768]{0:T(1024)(128)(4,1)S(1)} %iota_compare_fusion.1), kind=kOutput, calls=%fused_computation.2 | convolution fusion | flops 1411907584 | bytes 6620164 | tf_op jit(solution)/shard_map/dot_general | solution.py:25
  238.9 5.1 %stack.35 = f32[8]{0:T(128)S(1)} concatenate(f32[1]{0:T(128)} %bitcast.1, f32[1]{0:T(128)} %bitcast.3, f32[1]{0:T(128)} %bitcast.5, f32[1]{0:T(128)} %bitcast.7, f32[1]{0:T(128)} %bitcast.9, f32[1]{0:T(128)} %bitcast.11, f32[1]{0:T(128)} %bitcast.13, f32[1]{0:T(128)} %bitcast.15), dimensions={0} | concatenate | bytes 64 | tf_op jit(solution)/shard_map/stack | solution.py:30
  244.0 74.9 %psum.7 = f32[8]{0:T(128)S(1)} all-reduce(f32[8]{0:T(128)S(1)} %stack.35), channel_id=1, replica_groups=mesh['row'=32,'col'=8] {'row','col'}, use_global_device_ids=true, to_apply=%region_8.9 | all-reduce | flops 8 | bytes 64 | tf_op jit(solution)/shard_map/psum | solution.py:30
  318.9 0.5 add_divide_fusion
  319.5 0.7 fusion.41
  320.1 15.4 %fusion = bf16[896,1024]{0,1:T(8,128)(2,1)S(1)} fusion(f32[1024,896]{1,0:T(8,128)} %get-tuple-element.37, f32[]{:T(128)} %bitcast.23, f32[1024,896]{1,0:T(8,128)} %get-tuple-element.35, f32[]{:T(128)} %bitcast.22, f32[1024,896]{1,0:T(8,128)} %get-tuple-element.33, f32[]{:T(128)} %bitcast.21, f32[1024,896]{1,0:T(8,128)} %get-tuple-element.31, f32[]{:T(128)} %bitcast.20, ...), kind=kLoop, calls=%fused_computation.9 | loop fusion | flops 15597568 | bytes 31195168 | tf_op jit(solution)/shard_map/convert_element_type | solution.py:37
  335.6 2.4 copy.5
Async XLA Ops:
  7.2 70.2 %all-gather.5.cloned.1.call-start = ((), (), s32[]{:S(2)}) async-start(), calls=%async_computation.1 | async-start | bytes 12386304 | tf_op jit(solution)/shard_map/all_gather | solution.py:17
  7.9 191.3 %all-gather.3.cloned.1.call-start = ((), (), s32[]{:S(2)}) async-start(), calls=%async_computation | async-start | bytes 12976128 | tf_op jit(solution)/shard_map/all_gather | solution.py:18
  199.2 6.8 %copy-start = (bf16[6144,1024]{1,0:T(8,128)(2,1)S(1)}, bf16[6144,1024]{1,0:T(8,128)(2,1)}, u32[]{:S(2)}) copy-start(bf16[6144,1024]{1,0:T(8,128)(2,1)} %all-gather.3.cloned.1.call-done) | copy-start | bytes 37748740
  206.0 5.9 %copy-start.1 = (bf16[6144,896]{1,0:T(8,128)(2,1)S(1)}, bf16[6144,896]{1,0:T(8,128)(2,1)}, u32[]{:S(2)}) copy-start(bf16[6144,896]{1,0:T(8,128)(2,1)} %all-gather.5.cloned.1.call-done) | copy-start | bytes 33030148
Sparse Core Ops, SparseCore 0:
  9.8 67.4 all-gather.4
  79.9 119.2 all-gather.2
where the time goes:
time: 345 us
  waiting for transfers between devices  185 us (54%)
  blocking collectives  74.9 us (22%)
  matrix products  39.3 us (11%)
  other arithmetic  20.9 us (6%)
  between operations  14.1 us (4%)
  local copies, waits for them, and re-layouts  10.2 us (3%)
    all_gather x1, waiting for transfers between devices, body(): grad_full = lax.all_gather(out_grad, 'row', axis=0, tiled=True)  122 us
    psum x1, blocking collectives, body(): squares = lax.psum(jnp.stack(locals_), ('row', 'col'))  74.9 us
    all_gather x1, waiting for transfers between devices, body(): act_full = lax.all_gather(acts, 'col', axis=0, tiled=True)  62 us
    dot_general x8, matrix products, body(): lax.dot_general(act_rows, grad_rows, (((0,), (0,)), ((), ())), preferred_...  39.3 us
    convert_element_type x1, other arithmetic, body(): weight_grad = (total / jnp.sqrt(jnp.float32(tokens))).astype(jnp.bfloat16)  15.4 us
  transfers between devices with their start and end apart: 2, of which 2 were waited for; matrix products, arithmetic and copies ran while one was open for 2% of the time, Pallas kernels for 0%

commit v1 on v0

--- a/solution.py
+++ b/solution.py
@@ -14,7 +14,15 @@
     seqs = lengths.shape[0]
     seq_len = tokens // seqs
     slot = lax.broadcasted_iota(jnp.int32, (seq_len, 1), 0)
-    act_full = lax.all_gather(acts, "col", axis=0, tiled=True)
+    lanes = lax.axis_size("col")
+    block_out = acts
+    entries = [block_out]
+    u_next = [(m - 1, m) for m in range(1, lanes)] + [(lanes - 1, 0)]
+    for _ in range(lanes - 1):
+        block_out = lax.ppermute(block_out, "col", u_next)
+        entries += [block_out]
+    piece_next = jnp.concatenate([*reversed(entries)], 0)
+    act_full = jnp.roll(piece_next, (lax.axis_index("col") + 1) * block_out.shape[0], axis=0)
     grad_full = lax.all_gather(out_grad, "row", axis=0, tiled=True)
     products = []
     locals_ = []

time: 345 us -> 325 us (0.942)
  waiting for transfers between devices: 185 us -> 101 us
  local copies, waits for them, and re-layouts: 10.2 us -> 35.5 us
  starting transfers between devices: 0.08 us -> 17.5 us
  blocking collectives: 74.9 us -> 87.7 us
  matrix products: 39.3 us -> 45.2 us
    all_gather x1, waiting for transfers between devices: 122 us -> 0.01 us  [body(): grad_full = lax.all_gather(out_grad, 'row', axis=0, tiled=True)]
    ppermute x0 -> x7, waiting for transfers between devices: none -> 101 us  [body(): block_out = lax.ppermute(block_out, 'col', u_next)]
    all_gather x1 -> x0, waiting for transfers between devices: 62 us -> none  [body(): act_full = lax.all_gather(acts, 'col', axis=0, tiled=True)]
    unnamed x5 -> x35, local copies, waits for them, and re-layouts: 2.84 us -> 26.9 us
    ppermute x0 -> x7, starting transfers between devices: none -> 17.5 us  [body(): block_out = lax.ppermute(block_out, 'col', u_next)]
    psum x1, blocking collectives: 74.9 us -> 87.7 us  [body(): squares = lax.psum(jnp.stack(locals_), ('row', 'col'))]
    dot_general x8, matrix products: 39.3 us -> 45.2 us  [body(): lax.dot_general(act_rows, grad_rows, (((0,), (0,)), ((), ())), preferred_...]
  transfers between devices with their start and end apart: 2 -> 8, of which waited for: 2 -> 7; matrix products, arithmetic and copies ran while one was open for 2% -> 10% of each run, Pallas kernels for 0% -> 0%
where the time goes in v1:
time: 325 us
  waiting for transfers between devices  101 us (31%)
  blocking collectives  87.7 us (27%)
  matrix products  45.2 us (14%)
  local copies, waits for them, and re-layouts  35.5 us (11%)
  other arithmetic  23.1 us (7%)
  starting transfers between devices  17.5 us (5%)
  between operations  14.1 us (4%)
    ppermute x7, waiting for transfers between devices, body(): block_out = lax.ppermute(block_out, 'col', u_next)  101 us
    psum x1, blocking collectives, body(): squares = lax.psum(jnp.stack(locals_), ('row', 'col'))  87.7 us
    dot_general x8, matrix products, body(): lax.dot_general(act_rows, grad_rows, (((0,), (0,)), ((), ())), preferred_...  45.2 us
    unnamed x35, local copies, waits for them, and re-layouts  26.9 us
    convert_element_type x1, other arithmetic, body(): weight_grad = (total / jnp.sqrt(jnp.float32(tokens))).astype(jnp.bfloat16)  17.6 us
    ppermute x7, starting transfers between devices, body(): block_out = lax.ppermute(block_out, 'col', u_next)  17.5 us
  transfers between devices with their start and end apart: 8, of which 7 were waited for; matrix products, arithmetic and copies ran while one was open for 10% of the time, Pallas kernels for 0%

profile of v1, /device:TPU:1, one launch (start us, length us, event | category | flops | bytes accessed | tf_op | source)
XLA Modules:
  0.0 324.6 jit_solution(15030945668532102172)
XLA Ops:
  7.2 0.7 all-gather.2.cloned.1.call-update
  7.9 2.6 collective-permute-start
  10.5 15.6 %collective-permute-done = bf16[768,896]{1,0:T(8,128)(2,1)S(1)} collective-permute-done((bf16[768,896]{1,0:T(8,128)(2,1)}, bf16[768,896]{1,0:T(8,128)(2,1)S(1)}, u32[]{:S(2)}, u32[]{:S(2)}) %collective-permute-start) | collective-permute-done | bytes 1376288 | tf_op jit(solution)/shard_map/ppermute | solution.py:22
  26.1 2.4 collective-permute-start.1
  28.5 15.3 %collective-permute-done.1 = bf16[768,896]{1,0:T(8,128)(2,1)S(1)} collective-permute-done((bf16[768,896]{1,0:T(8,128)(2,1)S(1)}, bf16[768,896]{1,0:T(8,128)(2,1)S(1)}, u32[]{:S(2)}, u32[]{:S(2)}) %collective-permute-start.1) | collective-permute-done | bytes 1376288 | tf_op jit(solution)/shard_map/ppermute | solution.py:22
  43.7 2.5 collective-permute-start.2
  46.2 15.3 %collective-permute-done.2 = bf16[768,896]{1,0:T(8,128)(2,1)S(1)} collective-permute-done((bf16[768,896]{1,0:T(8,128)(2,1)S(1)}, bf16[768,896]{1,0:T(8,128)(2,1)S(1)}, u32[]{:S(2)}, u32[]{:S(2)}) %collective-permute-start.2) | collective-permute-done | bytes 1376288 | tf_op jit(solution)/shard_map/ppermute | solution.py:22
  61.4 1.1 copy-done.1
  62.5 2.5 collective-permute-start.3
  65.0 15.3 %collective-permute-done.3 = bf16[768,896]{1,0:T(8,128)(2,1)S(1)} collective-permute-done((bf16[768,896]{1,0:T(8,128)(2,1)S(1)}, bf16[768,896]{1,0:T(8,128)(2,1)S(1)}, u32[]{:S(2)}, u32[]{:S(2)}) %collective-permute-start.3) | collective-permute-done | bytes 1376288 | tf_op jit(solution)/shard_map/ppermute | solution.py:22
  80.3 1.1 copy-done.3
  81.3 2.5 collective-permute-start.4
  83.8 15.3 %collective-permute-done.4 = bf16[768,896]{1,0:T(8,128)(2,1)S(1)} collective-permute-done((bf16[768,896]{1,0:T(8,128)(2,1)S(1)}, bf16[768,896]{1,0:T(8,128)(2,1)S(1)}, u32[]{:S(2)}, u32[]{:S(2)}) %collective-permute-start.4) | collective-permute-done | bytes 1376288 | tf_op jit(solution)/shard_map/ppermute | solution.py:22
  99.1 1.1 copy-done.5
  100.1 2.5 collective-permute-start.5
  102.6 15.3 %collective-permute-done.5 = bf16[768,896]{1,0:T(8,128)(2,1)} collective-permute-done((bf16[768,896]{1,0:T(8,128)(2,1)S(1)}, bf16[768,896]{1,0:T(8,128)(2,1)}, u32[]{:S(2)}, u32[]{:S(2)}) %collective-permute-start.5) | collective-permute-done | bytes 1376288 | tf_op jit(solution)/shard_map/ppermute | solution.py:22
  117.9 2.6 collective-permute-start.6
  120.5 1.6 fusion.49
  125.1 0.7 iota_compare_fusion.3
  127.1 8.9 %collective-permute-done.6 = bf16[768,896]{1,0:T(8,128)(2,1)} collective-permute-done((bf16[768,896]{1,0:T(8,128)(2,1)}, bf16[768,896]{1,0:T(8,128)(2,1)}, u32[]{:S(2)}, u32[]{:S(2)}) %collective-permute-start.6) | collective-permute-done | bytes 1376288 | tf_op jit(solution)/shard_map/ppermute | solution.py:22
  136.0 2.6 constant_dynamic-update-slice_fusion.15
  138.6 2.6 constant_dynamic-update-slice_fusion.14
  141.2 1.2 constant_dynamic-update-slice_fusion.13
  142.4 1.2 constant_dynamic-update-slice_fusion.12
  143.6 1.2 constant_dynamic-update-slice_fusion.11
  144.9 1.2 constant_dynamic-update-slice_fusion.10
  146.1 1.3 constant_dynamic-update-slice_fusion.9
  147.4 1.2 constant_dynamic-update-slice_fusion.8
  148.6 2.5 constant_dynamic-update-slice_fusion.7
  151.1 2.6 constant_dynamic-update-slice_fusion.6
  153.7 1.2 constant_dynamic-update-slice_fusion.5
  154.9 1.2 constant_dynamic-update-slice_fusion.4
  156.1 1.2 constant_dynamic-update-slice_fusion.3
  157.3 1.2 constant_dynamic-update-slice_fusion.2
  158.5 1.2 constant_dynamic-update-slice_fusion.1
  159.7 1.2 constant_dynamic-update-slice_fusion
  160.9 6.1 %multiply_reduce_fusion.7 = (f32[]{:T(128)}, f32[896,1024]{1,0:T(8,128)}) fusion(bf16[6144,1024]{1,0:T(8,128)(2,1)} %all-gather.2.cloned.1.call-done, pred[768]{0:T(1024)(128)(4,1)S(1)} %iota_compare_fusion.7, bf16[12288,896]{1,0:T(8,128)(2,1)} %constant_dynamic-update-slice_fusion, s32[]{:T(128)S(6)} %select_n.39), kind=kOutput, calls=%fused_computation.8 | convolution fusion | flops 1411907584 | bytes 6619912 | tf_op jit(solution)/shard_map/dot_general | solution.py:33
  167.1 6.1 %multiply_reduce_fusion.2 = (f32[]{:T(128)}, f32[896,1024]{1,0:T(8,128)}) fusion(bf16[6144,1024]{1,0:T(8,128)(2,1)} %all-gather.2.cloned.1.call-done, pred[768]{0:T(1024)(128)(4,1)S(1)} %iota_compare_fusion.2, bf16[12288,896]{1,0:T(8,128)(2,1)} %constant_dynamic-update-slice_fusion, s32[]{:T(128)S(6)} %add.54), kind=kOutput, calls=%fused_computation.3 | convolution fusion | flops 1411907584 | bytes 6619912 | tf_op jit(solution)/shard_map/dot_general | solution.py:33
  173.2 5.5 %multiply_reduce_fusion.1 = (f32[]{:T(128)}, f32[896,1024]{1,0:T(8,128)}) fusion(bf16[6144,1024]{1,0:T(8,128)(2,1)S(1)} %bitcast.25, pred[768]{0:T(1024)(128)(4,1)S(1)} %iota_compare_fusion.1, bf16[12288,896]{1,0:T(8,128)(2,1)} %constant_dynamic-update-slice_fusion, s32[]{:T(128)S(6)} %add.55), kind=kOutput, calls=%fused_computation.2 | convolution fusion | flops 1411907584 | bytes 6620168 | tf_op jit(solution)/shard_map/dot_general | solution.py:33
  178.7 5.5 %multiply_reduce_fusion.6 = (f32[]{:T(128)}, f32[896,1024]{1,0:T(8,128)}) fusion(bf16[6144,1024]{1,0:T(8,128)(2,1)S(1)} %bitcast.25, pred[768]{0:T(1024)(128)(4,1)S(1)} %iota_compare_fusion.6, bf16[12288,896]{1,0:T(8,128)(2,1)} %constant_dynamic-update-slice_fusion, s32[]{:T(128)S(6)} %add.50), kind=kOutput, calls=%fused_computation.7 | convolution fusion | flops 1411907584 | bytes 6620168 | tf_op jit(solution)/shard_map/dot_general | solution.py:33
  184.2 5.5 %multiply_reduce_fusion.5 = (f32[]{:T(128)}, f32[896,1024]{1,0:T(8,128)}) fusion(bf16[6144,1024]{1,0:T(8,128)(2,1)S(1)} %bitcast.25, pred[768]{0:T(1024)(128)(4,1)S(1)} %iota_compare_fusion.5, bf16[12288,896]{1,0:T(8,128)(2,1)} %constant_dynamic-update-slice_fusion, s32[]{:T(128)S(6)} %add.51), kind=kOutput, calls=%fused_computation.6 | convolution fusion | flops 1411907584 | bytes 6620168 | tf_op jit(solution)/shard_map/dot_general | solution.py:33
  189.7 5.6 %multiply_reduce_fusion.4 = (f32[]{:T(128)}, f32[896,1024]{1,0:T(8,128)}) fusion(bf16[6144,1024]{1,0:T(8,128)(2,1)S(1)} %bitcast.25, pred[768]{0:T(1024)(128)(4,1)S(1)} %iota_compare_fusion.4, bf16[12288,896]{1,0:T(8,128)(2,1)} %constant_dynamic-update-slice_fusion, s32[]{:T(128)S(6)} %add.52), kind=kOutput, calls=%fused_computation.5 | convolution fusion | flops 1411907584 | bytes 6620168 | tf_op jit(solution)/shard_map/dot_general | solution.py:33
  195.3 5.4 %multiply_reduce_fusion.3 = (f32[]{:T(128)}, f32[896,1024]{1,0:T(8,128)}) fusion(bf16[6144,1024]{1,0:T(8,128)(2,1)S(1)} %bitcast.25, pred[768]{0:T(1024)(128)(4,1)S(1)} %iota_compare_fusion.3, bf16[12288,896]{1,0:T(8,128)(2,1)} %constant_dynamic-update-slice_fusion, s32[]{:T(128)S(6)} %add.53), kind=kOutput, calls=%fused_computation.4 | convolution fusion | flops 1411907584 | bytes 6620168 | tf_op jit(solution)/shard_map/dot_general | solution.py:33
  200.7 5.5 %multiply_reduce_fusion = (f32[]{:T(128)}, f32[896,1024]{1,0:T(8,128)}) fusion(bf16[6144,1024]{1,0:T(8,128)(2,1)S(1)} %bitcast.25, pred[768]{0:T(1024)(128)(4,1)S(1)} %iota_compare_fusion, bf16[12288,896]{1,0:T(8,128)(2,1)} %constant_dynamic-update-slice_fusion, s32[]{:T(128)S(6)} %add.56), kind=kOutput, calls=%fused_computation.1 | convolution fusion | flops 1411907584 | bytes 6620168 | tf_op jit(solution)/shard_map/dot_general | solution.py:33
  206.2 5.1 %stack.35 = f32[8]{0:T(128)S(1)} concatenate(f32[1]{0:T(128)} %bitcast.1, f32[1]{0:T(128)} %bitcast.3, f32[1]{0:T(128)} %bitcast.5, f32[1]{0:T(128)} %bitcast.7, f32[1]{0:T(128)} %bitcast.9, f32[1]{0:T(128)} %bitcast.11, f32[1]{0:T(128)} %bitcast.13, f32[1]{0:T(128)} %bitcast.15), dimensions={0} | concatenate | bytes 64 | tf_op jit(solution)/shard_map/stack | solution.py:38
  211.2 87.7 %psum.7 = f32[8]{0:T(128)S(1)} all-reduce(f32[8]{0:T(128)S(1)} %stack.35), channel_id=1, replica_groups=mesh['row'=32,'col'=8] {'row','col'}, use_global_device_ids=true, to_apply=%region_8.9 | all-reduce | flops 8 | bytes 64 | tf_op jit(solution)/shard_map/psum | solution.py:38
  299.5 0.7 fusion.48
  300.2 17.6 %multiply_convert_fusion = bf16[896,1024]{1,0:T(8,128)(2,1)} fusion(f32[896,1024]{1,0:T(8,128)} %get-tuple-element.35, f32[896,1024]{1,0:T(8,128)} %get-tuple-element.33, f32[896,1024]{1,0:T(8,128)} %get-tuple-element.31, f32[896,1024]{1,0:T(8,128)} %get-tuple-element.29, f32[896,1024]{1,0:T(8,128)} %get-tuple-element.27, f32[896,1024]{1,0:T(8,128)} %get-tuple-element.25, ...), kind=kLoop, calls=%fused_computation | loop fusion | flops 15597568 | bytes 31195168 | tf_op jit(solution)/shard_map/convert_element_type | solution.py:45
  (28 shorter events, 4.9 us)
Async XLA Ops:
  7.2 153.8 %all-gather.2.cloned.1.call-start = ((), (), s32[]{:S(2)}) async-start(), calls=%async_computation | async-start | bytes 12976128 | tf_op jit(solution)/shard_map/all_gather | solution.py:26
  7.9 18.2 %collective-permute-start = (bf16[768,896]{1,0:T(8,128)(2,1)}, bf16[768,896]{1,0:T(8,128)(2,1)S(1)}, u32[]{:S(2)}, u32[]{:S(2)}) collective-permute-start(bf16[768,896]{1,0:T(8,128)(2,1)} %param.3), channel_id=1, source_target_pairs={{0,1},{1,2},{2,3},{3,4},{4,5},{5,6},{6,7},{7,0},{8,9},{9,10},{10,1... | collective-permute-start | bytes 4128776 | tf_op jit(solution)/shard_map/ppermute | solution.py:22
  26.1 17.6 %collective-permute-start.1 = (bf16[768,896]{1,0:T(8,128)(2,1)S(1)}, bf16[768,896]{1,0:T(8,128)(2,1)S(1)}, u32[]{:S(2)}, u32[]{:S(2)}) collective-permute-start(bf16[768,896]{1,0:T(8,128)(2,1)S(1)} %collective-permute-done), channel_id=1, source_target_pairs={{0,1},{1,2},{2,3},{3,4},{4,5},{5,6},{6,7},{7,0},{8,9},{9,10},{10,1... | collective-permute-start | bytes 4128776 | tf_op jit(solution)/shard_map/ppermute | solution.py:22
  43.7 17.7 %collective-permute-start.2 = (bf16[768,896]{1,0:T(8,128)(2,1)S(1)}, bf16[768,896]{1,0:T(8,128)(2,1)S(1)}, u32[]{:S(2)}, u32[]{:S(2)}) collective-permute-start(bf16[768,896]{1,0:T(8,128)(2,1)S(1)} %collective-permute-done.1), channel_id=1, source_target_pairs={{0,1},{1,2},{2,3},{3,4},{4,5},{5,6},{6,7},{7,0},{8,9},{9,10},{10,1... | collective-permute-start | bytes 4128776 | tf_op jit(solution)/shard_map/ppermute | solution.py:22
  61.4 1.1 copy-start.1
  62.5 17.7 %collective-permute-start.3 = (bf16[768,896]{1,0:T(8,128)(2,1)S(1)}, bf16[768,896]{1,0:T(8,128)(2,1)S(1)}, u32[]{:S(2)}, u32[]{:S(2)}) collective-permute-start(bf16[768,896]{1,0:T(8,128)(2,1)S(1)} %collective-permute-done.2), channel_id=1, source_target_pairs={{0,1},{1,2},{2,3},{3,4},{4,5},{5,6},{6,7},{7,0},{8,9},{9,10},{10,1... | collective-permute-start | bytes 4128776 | tf_op jit(solution)/shard_map/ppermute | solution.py:22
  80.3 1.1 copy-start.3
  81.3 17.7 %collective-permute-start.4 = (bf16[768,896]{1,0:T(8,128)(2,1)S(1)}, bf16[768,896]{1,0:T(8,128)(2,1)S(1)}, u32[]{:S(2)}, u32[]{:S(2)}) collective-permute-start(bf16[768,896]{1,0:T(8,128)(2,1)S(1)} %collective-permute-done.3), channel_id=1, source_target_pairs={{0,1},{1,2},{2,3},{3,4},{4,5},{5,6},{6,7},{7,0},{8,9},{9,10},{10,1... | collective-permute-start | bytes 4128776 | tf_op jit(solution)/shard_map/ppermute | solution.py:22
  99.1 1.1 copy-start.5
  100.1 17.7 %collective-permute-start.5 = (bf16[768,896]{1,0:T(8,128)(2,1)S(1)}, bf16[768,896]{1,0:T(8,128)(2,1)}, u32[]{:S(2)}, u32[]{:S(2)}) collective-permute-start(bf16[768,896]{1,0:T(8,128)(2,1)S(1)} %collective-permute-done.4), channel_id=1, source_target_pairs={{0,1},{1,2},{2,3},{3,4},{4,5},{5,6},{6,7},{7,0},{8,9},{9,10},{10,1... | collective-permute-start | bytes 4128776 | tf_op jit(solution)/shard_map/ppermute | solution.py:22
  117.9 18.2 %collective-permute-start.6 = (bf16[768,896]{1,0:T(8,128)(2,1)}, bf16[768,896]{1,0:T(8,128)(2,1)}, u32[]{:S(2)}, u32[]{:S(2)}) collective-permute-start(bf16[768,896]{1,0:T(8,128)(2,1)} %collective-permute-done.5), channel_id=1, source_target_pairs={{0,1},{1,2},{2,3},{3,4},{4,5},{5,6},{6,7},{7,0},{8,9},{9,10},{10,1... | collective-permute-start | bytes 4128776 | tf_op jit(solution)/shard_map/ppermute | solution.py:22
  120.5 20.8 %copy-start.6 = (bf16[768,896]{1,0:T(8,128)(2,1)S(1)}, bf16[768,896]{1,0:T(8,128)(2,1)}, u32[]{:S(2)}) copy-start(bf16[768,896]{1,0:T(8,128)(2,1)} %copy-done.5) | copy-start | bytes 4128772
  127.1 15.3 %copy-start.4 = (bf16[768,896]{1,0:T(8,128)(2,1)S(1)}, bf16[768,896]{1,0:T(8,128)(2,1)}, u32[]{:S(2)}) copy-start(bf16[768,896]{1,0:T(8,128)(2,1)} %copy-done.3) | copy-start | bytes 4128772
  138.6 5.0 %copy-start.2 = (bf16[768,896]{1,0:T(8,128)(2,1)S(1)}, bf16[768,896]{1,0:T(8,128)(2,1)}, u32[]{:S(2)}) copy-start(bf16[768,896]{1,0:T(8,128)(2,1)} %copy-done.1) | copy-start | bytes 4128772
  143.6 3.7 %copy-start = (bf16[768,896]{1,0:T(8,128)(2,1)S(1)}, bf16[768,896]{1,0:T(8,128)(2,1)}, u32[]{:S(2)}) copy-start(bf16[768,896]{1,0:T(8,128)(2,1)} %param.3) | copy-start | bytes 4128772
  160.9 12.2 %slice-start = ((s8[12582912]{0:T(1024)(128)(4,1)}), s8[4194304]{0:T(1024)(128)(4,1)S(1)}, s32[]{:S(2)}) async-start(s8[12582912]{0:T(1024)(128)(4,1)} %bitcast.24), calls=%async_computation.1 | async-start | bytes 8388608
  160.9 12.2 %slice-start.1 = ((s8[12582912]{0:T(1024)(128)(4,1)}), s8[4194304]{0:T(1024)(128)(4,1)S(1)}, s32[]{:S(2)}) async-start(s8[12582912]{0:T(1024)(128)(4,1)} %bitcast.24), calls=%async_computation.2 | async-start | bytes 8388608
  167.1 6.1 %slice-start.2 = ((s8[12582912]{0:T(1024)(128)(4,1)}), s8[4194304]{0:T(1024)(128)(4,1)S(1)}, s32[]{:S(2)}) async-start(s8[12582912]{0:T(1024)(128)(4,1)} %bitcast.24), calls=%async_computation.3 | async-start | bytes 8388608
Sparse Core Ops, SparseCore 0:
  10.6 123.1 all-gather.1
